TPU v7x, 32 devices: a whole 2x2x4 slice. The times are simulated.
32 devices in a mesh: kz: 4 (over x, core), tile: 8 (over z, y).
Axes of the slice: x: 2, y: 2, z: 4, core: 2. Of those that a mesh axis runs over, the one named last changes fastest.
Arguments:
- coil_data: bfloat16 [4, 8, 4, 8, 2, 16, 128], P('kz', 'tile'), may hold values from -6 to 6
- frame_of: int32 [4, 8, 4, 8, 2], P('kz', 'tile'), may hold values from 0 to 999
- basis: bfloat16 [1000, 10], replicated, may hold values from -4 to 4
- sample_pos: float32 [4, 8, 4, 8, 2, 2, 128], P('kz', 'tile'), may hold values from 1.5 to 30.5, as said below
- window_at: int32 [4, 8, 4, 8, 2, 2], P('kz', 'tile'), may hold values from -2 to 639, as said below
- live_count: int32 [4, 8, 4, 8], P('kz', 'tile'), may hold values from 0 to 2, as said below
Outputs:
- image: bfloat16 [4, 640, 102400], P('kz', None, 'tile')
Inputs may be any that keep to these rules, and one draw needn't show every extreme that they name: `live_count`: live slots of a pair are its first ones; destination tiles from 3 up to but not including 8 * 5 // 8 receive every slot from every acquiring device. `window_at`: the first entry (row0) lies in -2 to 78, the second (col0) in 0 to 639. `sample_pos`: the first entry lies in 1.5 to 2.5, the second in 1.5 to 32 - 1.5.
All inputs are finite; a program needn't handle non-finite values.
Results may differ from a plain program's by a relative error of at most 0.0077.
Values may be sent and summed in bfloat16 or wider, within the bound.
No kernel may reach another device: no remote copies, remote signals or barrier semaphores. Data moves between devices by JAX's collectives and lax.ppermute only.
A program may use at most 192 MiB of HBM per device.

v0:
```python
import math

import jax
import jax.numpy as jnp
from jax import lax
from jax.sharding import PartitionSpec as P

PLANE = 640
WIN_ROWS = 4
WIN_COLS = 32


def from_behind(value, axis, steps):
    count = lax.axis_size(axis)
    pairs = [(source, (source + steps) % count) for source in range(count)]
    return lax.ppermute(value, axis, pairs)


def taper(dist):
    inner = 1.0 - (dist / 1.5) ** 2
    return jnp.maximum(inner, 0.0) ** 2


def project(blocks, coeffs):
    count = blocks.shape[0]
    coils = blocks.shape[1] // 2
    ranks = coeffs.shape[1]
    samples = blocks.shape[2]
    data = blocks.astype(jnp.float32).reshape(count, 2, 1, coils, samples)
    scale = coeffs.astype(jnp.float32).reshape(count, 1, ranks, 1, 1)
    return (data * scale).reshape(count, 2 * ranks * coils, samples).astype(jnp.bfloat16)


def grid_tile(proj, offsets, corners, alive, tile_rows, plane):
    count, width, samples = proj.shape
    group = 64
    row_cells = jnp.arange(WIN_ROWS, dtype=jnp.float32)
    col_cells = jnp.arange(WIN_COLS, dtype=jnp.float32)
    cells = jnp.arange(WIN_ROWS * WIN_COLS, dtype=jnp.int32)
    cell_row = cells // WIN_COLS
    cell_col = cells % WIN_COLS

    def step(acc, items):
        values, place, corner, living = items
        row_k = taper(row_cells[None, :, None] - place[:, 0:1, :])
        col_k = taper(col_cells[None, :, None] - place[:, 1:2, :])
        weights = (row_k[:, :, None, :] * col_k[:, None, :, :]).reshape(
            group, WIN_ROWS * WIN_COLS, samples
        )
        weights = (weights * living[:, None, None]).astype(jnp.bfloat16)
        contrib = jnp.einsum("gwb,gcb->gwc", weights, values, preferred_element_type=jnp.float32)
        rows = corner[:, 0:1] + 2 + cell_row[None, :]
        cols = (corner[:, 1:2] + cell_col[None, :]) % plane
        acc = acc.at[rows.reshape(-1), cols.reshape(-1)].add(contrib.reshape(-1, width))
        return (acc, None)

    start = jnp.zeros((tile_rows + 4, plane, width), jnp.float32)
    items = (
        proj.reshape(-1, group, width, samples),
        offsets.reshape(-1, group, 2, samples),
        corners.reshape(-1, group, 2),
        alive.reshape(-1, group),
    )
    acc, _ = lax.scan(step, start, items)
    return acc


def tables(n):
    idx = jnp.arange(n, dtype=jnp.int32)
    phase = (idx[:, None] * idx[None, :] % n).astype(jnp.float32) * (2.0 * math.pi / n)
    return (jnp.cos(phase).astype(jnp.bfloat16), jnp.sin(phase).astype(jnp.bfloat16))


def combine(first, second, half):
    return jnp.concatenate(
        [first[..., :half] - second[..., half:], second[..., :half] + first[..., half:]], axis=-1
    )


def body(coil_data, frame_of, basis, sample_pos, window_at, live_count):
    parts = coil_data.shape[2]
    tiles = coil_data.shape[3]
    slots = coil_data.shape[4]
    pair = coil_data.shape[5]
    samples = coil_data.shape[6]
    width = 2 * basis.shape[1] * (pair // 2)
    half = width // 2
    tile_rows = PLANE // tiles
    raw = lax.all_to_all(
        lax.all_to_all(coil_data, "kz", split_axis=2, concat_axis=0, tiled=True),
        "tile",
        split_axis=3,
        concat_axis=1,
        tiled=True,
    )
    frames = lax.all_to_all(
        lax.all_to_all(frame_of, "kz", split_axis=2, concat_axis=0, tiled=True),
        "tile",
        split_axis=3,
        concat_axis=1,
        tiled=True,
    )
    arrived = project(raw.reshape(-1, pair, samples), basis[frames.reshape(-1)])
    slot_idx = jnp.arange(slots, dtype=jnp.int32)
    counts = live_count.reshape(parts, tiles)
    alive = (slot_idx[None, None, :] < counts[:, :, None]).astype(jnp.float32)
    acc = grid_tile(
        arrived,
        sample_pos.reshape(-1, 2, samples),
        window_at.reshape(-1, 2),
        alive.reshape(-1),
        tile_rows,
        PLANE,
    )
    from_above = from_behind(acc[tile_rows + 2 : tile_rows + 4], "tile", 1)
    from_below = from_behind(acc[0:2], "tile", -1)
    core = acc[2 : tile_rows + 2]
    core = core.at[0:2].add(from_above)
    core = core.at[tile_rows - 2 : tile_rows].add(from_below)
    grid = core.astype(jnp.bfloat16)
    cos_tab, sin_tab = tables(PLANE)
    first = jnp.einsum("xkq,ky->xyq", grid, cos_tab, preferred_element_type=jnp.float32)
    second = jnp.einsum("xkq,ky->xyq", grid, sin_tab, preferred_element_type=jnp.float32)
    mid = combine(first, second, half).astype(jnp.bfloat16)
    columns = lax.all_to_all(mid, "tile", split_axis=1, concat_axis=0, tiled=True)
    first = jnp.einsum("kyq,kx->xyq", columns, cos_tab, preferred_element_type=jnp.float32)
    second = jnp.einsum("kyq,kx->xyq", columns, sin_tab, preferred_element_type=jnp.float32)
    result = (combine(first, second, half) * (1.0 / PLANE)).astype(jnp.bfloat16)
    return result.reshape(1, result.shape[0], -1)


def solution(mesh):
    return jax.shard_map(
        body,
        mesh=mesh,
        in_specs=(
            P("kz", "tile", None, None, None, None, None),
            P("kz", "tile", None, None, None),
            P(),
            P("kz", "tile", None, None, None, None, None),
            P("kz", "tile", None, None, None, None),
            P("kz", "tile", None, None),
        ),
        out_specs=P("kz", None, "tile"),
        check_vma=False,
    )
```

profile of v0, /device:TPU:0, one launch (start us, length us, event | category | flops | bytes accessed | tf_op | source)
XLA Modules:
  0.0 1157.6 jit_solution(10622517823598696329)
XLA Ops:
  0.0 4.4 all-to-all-start.2
  19.8 6.3 all-to-all-start.3
  27.2 5.4 all-to-all-done.3
  37.2 7.0 all-to-all-done.1
  45.9 5.1 fusion.33
  51.1 66.7 %scatter_custom_fusion = f32[53760,160]{1,0:T(8,128)} fusion(s32[8192]{0:T(1024)S(1)} %broadcast_select_fusion, f32[8192,160]{1,0:T(8,128)} %bitcast.76, f32[]{:T(128)} %constant.134.clone.1), kind=kCustom, calls=%fused_computation.4 | custom fusion | flops 1310720 | bytes 34406912
  125.2 4.6 collective-permute-start.1
  129.7 34.4 %slice.123 = f32[51200,160]{1,0:T(8,128)} slice(f32[53760,160]{1,0:T(8,128)} %scatter_custom_fusion), slice={[1280:52480], [0:160]} | slice | bytes 65536000 | tf_op jit(solution)/shard_map/slice | solution.py:117
  165.0 52.2 %copy.108 = f32[80,640,160]{1,0,2:T(8,128)} copy(f32[80,640,160]{2,1,0:T(8,128)} %bitcast.66) | data formatting | bytes 65536000 | tf_op jit(solution)/shard_map/slice | solution.py:117
  223.1 11.5 convert_element_type.79
  234.6 9.7 copy.100
  244.3 30.4 %fusion.13 = f32[640,12800]{0,1} fusion(bf16[640,12800]{0,1:T(8,128)(2,1)} %bitcast.74), kind=kOutput, calls=%fused_computation.31 | convolution fusion | flops 10489856000 | bytes 49152000
  274.7 30.5 %fusion.15 = f32[640,12800]{0,1} fusion(bf16[640,12800]{0,1:T(8,128)(2,1)} %bitcast.75), kind=kOutput, calls=%fused_computation.33 | convolution fusion | flops 10489856000 | bytes 49152000
  305.2 24.4 %fusion.4 = (bf16[80,640,80]{1,2,0:T(8,128)(2,1)S(1)}, bf16[80,640,80]{1,2,0:T(8,128)(2,1)}) fusion(f32[80,640,160]{1,2,0:T(8,128)} %bitcast.71, f32[80,640,160]{1,2,0:T(8,128)} %bitcast.70), kind=kLoop, calls=%fused_computation.11 | loop fusion | flops 16384000 | bytes 81920000 | tf_op jit(solution)/shard_map/convert.2
  329.7 10.3 pad_maximum_fusion
  340.0 38.3 %copy.102 = bf16[80,640,160]{2,0,1:T(8,128)(2,1)} copy(bf16[80,640,160]{1,2,0:T(8,128)(2,1)} %pad_maximum_fusion) | data formatting | bytes 32768000 | tf_op jit(solution)/shard_map/concatenate | solution.py:75
  378.3 571.8 %all_to_all.60 = bf16[80,640,160]{2,0,1:T(8,128)(2,1)} all-to-all(bf16[80,640,160]{2,0,1:T(8,128)(2,1)} %copy.102), channel_id=1, replica_groups=mesh['kz'=4,'tile'=8] {'tile'}, dimensions={1} | all-to-all | bytes 32768000 | tf_op jit(solution)/shard_map/all_to_all | solution.py:125
  950.0 36.0 %copy.103 = bf16[80,8,80,160]{0,1,3,2:T(8,128)(2,1)} copy(bf16[80,8,80,160]{3,0,2,1:T(8,128)(2,1)} %bitcast.67) | data formatting | bytes 32768000 | tf_op jit(solution)/shard_map/all_to_all | solution.py:125
  986.0 37.6 %reshape.322 = bf16[640,12800]{0,1:T(8,128)(2,1)} reshape(bf16[8,80,80,160]{1,0,3,2:T(8,128)(2,1)} %bitcast.68) | data formatting | bytes 32768000
  1023.6 30.4 %fusion.14 = f32[640,12800]{0,1} fusion(bf16[640,12800]{0,1:T(8,128)(2,1)} %reshape.322), kind=kOutput, calls=%fused_computation.32 | convolution fusion | flops 10489856000 | bytes 49152000
  1054.0 30.6 %fusion.16 = f32[640,12800]{0,1} fusion(bf16[640,12800]{0,1:T(8,128)(2,1)} %reshape.322), kind=kOutput, calls=%fused_computation.34 | convolution fusion | flops 10489856000 | bytes 49152000
  1084.6 33.0 %slice_subtract_fusion = (f32[640,80,80]{0,2,1:T(8,128)}, f32[640,80,80]{0,2,1:T(8,128)}) fusion(f32[640,80,160]{0,2,1:T(8,128)} %bitcast.73, f32[640,80,160]{0,2,1:T(8,128)} %bitcast.72), kind=kLoop, calls=%fused_computation.7 | loop fusion | flops 8192000 | bytes 98304000 | tf_op jit(solution)/shard_map/sub | solution.py:76
  1117.6 17.7 %fusion = bf16[640,80,160]{0,2,1:T(8,128)(2,1)} fusion(f32[640,80,80]{0,2,1:T(8,128)} %get-tuple-element.60, f32[640,80,80]{0,2,1:T(8,128)} %get-tuple-element.59), kind=kLoop, calls=%fused_computation.3 | loop fusion | flops 24576000 | bytes 49152000 | tf_op jit(solution)/shard_map/convert_element_type | solution.py:128
  1135.3 21.9 %copy.104 = bf16[1,640,12800]{2,1,0:T(8,128)(2,1)} copy(bf16[1,640,12800]{1,2,0:T(8,128)(2,1)} %bitcast.69) | data formatting | bytes 32768000 | tf_op jit(solution)/shard_map/convert_element_type | solution.py:128
  (51 shorter events, 36.7 us)
Async XLA Ops:
  0.0 16.4 %copy-start.2 = (s32[2]{0:T(128)S(1)}, s32[2]{0:T(128)}, u32[]{:S(2)}) copy-start(s32[2]{0:T(128)} %constant.155) | copy-start | bytes 28
  0.0 26.1 %copy-start.1 = (s32[2]{0:T(128)S(1)}, s32[2]{0:T(128)}, u32[]{:S(2)}) copy-start(s32[2]{0:T(128)} %constant.152) | copy-start | bytes 28
  0.0 26.2 %copy-start = (bf16[1000,10]{0,1:T(8,128)(2,1)S(1)}, bf16[1000,10]{0,1:T(8,128)(2,1)}, u32[]{:S(2)}) copy-start(bf16[1000,10]{0,1:T(8,128)(2,1)} %param.12) | copy-start | bytes 60004
  0.0 10.3 all-to-all-start.2
  10.4 9.4 all-to-all-start
  19.8 12.9 %all-to-all-start.3 = ((s32[4,1,1,8,2]{0,4,2,1,3:T(2,128)}), s32[4,1,1,8,2]{0,4,2,1,3:T(2,128)S(1)}, u32[]{:S(2)}, u32[]{:S(2)}) async-start(s32[4,1,1,8,2]{0,4,2,1,3:T(2,128)} %copy.89), calls=%async_computation.3 | async-start | bytes 16384 | tf_op jit(solution)/shard_map/all_to_all | solution.py:96
  32.6 11.6 %all-to-all-start.1 = ((bf16[4,1,1,8,2,16,128]{6,5,4,0,2,1,3:T(8,128)(2,1)}), bf16[4,1,1,8,2,16,128]{6,5,4,0,2,1,3:T(8,128)(2,1)S(1)}, u32[]{:S(2)}, u32[]{:S(2)}) async-start(bf16[4,1,1,8,2,16,128]{6,5,4,0,2,1,3:T(8,128)(2,1)} %copy.85), calls=%async_computation.1 | async-start | bytes 524288 | tf_op jit(solution)/shard_map/all_to_all | solution.py:89
  123.6 93.5 %collective-permute-start = (f32[2,640,160]{1,0,2:T(2,128)}, f32[2,640,160]{1,0,2:T(2,128)}, u32[]{:S(2)}, u32[]{:S(2)}) collective-permute-start(f32[2,640,160]{1,0,2:T(2,128)} %copy.110), channel_id=1, source_target_pairs={{0,1},{1,2},{2,3},{3,4},{4,5},{5,6},{6,7},{7,0},{8,9},{9,10},{10,1... | collective-permute-start | bytes 2457608 | tf_op jit(solution)/shard_map/ppermute | solution.py:16
  125.2 94.6 %collective-permute-start.1 = (f32[2,640,160]{1,0,2:T(2,128)}, f32[2,640,160]{1,0,2:T(2,128)S(1)}, u32[]{:S(2)}, u32[]{:S(2)}) collective-permute-start(f32[2,640,160]{1,0,2:T(2,128)} %copy.111), channel_id=1, source_target_pairs={{0,7},{1,0},{2,1},{3,2},{4,3},{5,4},{6,5},{7,6},{8,15},{9,8},{10,9... | collective-permute-start | bytes 2457608 | tf_op jit(solution)/shard_map/ppermute | solution.py:16
where the time goes:
time: 1170 us; the launch traced here: 1160 us
  blocking collectives  572 us (49%)
  local copies, waits for them, and re-layouts  243 us (21%)
  other arithmetic  178 us (15%)
  matrix products  127 us (11%)
  starting transfers between devices  22.3 us (2%)
  waiting for transfers between devices  15 us (1%)
    all_to_all x1, blocking collectives, body(): lax.all_to_all(mid, 'tile', split_axis=1, concat_axis=0, tiled=True)  572 us
    unnamed x4, matrix products  122 us
    slice x2, local copies, waits for them, and re-layouts, body(): core = acc[2:tile_rows + 2]  86.6 us
    unnamed x4, other arithmetic  67 us
    unnamed x9, local copies, waits for them, and re-layouts  38.6 us
    concatenate x1, local copies, waits for them, and re-layouts, combine(): jnp.concatenate([first[..., :half] - second[..., half:], second[..., :hal...  38.3 us
    all_to_all x1, local copies, waits for them, and re-layouts, body(): lax.all_to_all(mid, 'tile', split_axis=1, concat_axis=0, tiled=True)  36 us
    sub x1, other arithmetic, combine(): first[..., :half] - second[..., half:]  33 us
  transfers between devices with their start and end apart: 6, of which 3 were waited for; matrix products, arithmetic and copies ran while one was open for 9% of the time, Pallas kernels for 0%

commit v1 on v0

v1 whole, which is shorter than its diff:
```python
import functools
import math

import jax
import jax.numpy as jnp
from jax import lax
from jax.experimental import pallas as pl
from jax.experimental.pallas import tpu as pltpu
from jax.sharding import PartitionSpec as P

PLANE = 640
WIN_ROWS = 4
WIN_COLS = 32
LANES = 128
META_KX = 64
NT_DIMS = (((1,), (1,)), ((), ()))


def taper(dist):
    inner = 1.0 - (dist * (1.0 / 1.5)) ** 2
    return jnp.maximum(inner, 0.0) ** 2


def phase_of(product):
    return (product % PLANE).astype(jnp.float32) * (2.0 * math.pi / PLANE)


def window_kernel(quad, data_ref, pos_ref, alive_ref, out_ref):
    _, pair, samples = data_ref.shape
    cols = lax.broadcasted_iota(jnp.int32, (WIN_COLS, samples), 0).astype(jnp.float32)
    row = lax.broadcasted_iota(jnp.int32, (quad * WIN_ROWS, samples), 0)
    spread = []
    weights = []
    for q in range(quad):
        place = pos_ref[q]
        col_k = taper(cols - place[1:2, :])
        data = data_ref[q].astype(jnp.float32)
        spread.append((col_k[:, None, :] * data[None, :, :]).reshape(WIN_COLS * pair, samples).astype(jnp.bfloat16))
        row_k = taper((row - q * WIN_ROWS).astype(jnp.float32) - place[0:1, :]) * alive_ref[q]
        mine = (row >= q * WIN_ROWS) & (row < (q + 1) * WIN_ROWS)
        weights.append(jnp.where(mine, row_k, 0.0).astype(jnp.bfloat16))
    out_ref[...] = lax.dot_general(
        jnp.concatenate(weights, axis=1), jnp.concatenate(spread, axis=1), NT_DIMS,
        preferred_element_type=jnp.float32,
    ).astype(jnp.bfloat16)


def grid_windows(raw, pos, alive):
    count, pair, samples = raw.shape
    quad = 4
    width = WIN_COLS * pair
    return pl.pallas_call(
        functools.partial(window_kernel, quad),
        grid=(count // quad,),
        in_specs=[
            pl.BlockSpec((quad, pair, samples), lambda s: (s, 0, 0)),
            pl.BlockSpec((quad, 2, samples), lambda s: (s, 0, 0)),
            pl.BlockSpec((quad, 1, samples), lambda s: (s, 0, 0)),
        ],
        out_specs=pl.BlockSpec((quad * WIN_ROWS, width), lambda s: (s, 0)),
        out_shape=jax.ShapeDtypeStruct((count * WIN_ROWS, width), jnp.bfloat16),
        name="grid_windows",
    )(raw, pos, jnp.broadcast_to(alive[:, None, None], (count, 1, samples)))


def columns_kernel(coils, grid_ref, table_ref, turn_ref, out_ref):
    rows, _ = table_ref.shape
    depth = grid_ref.shape[1]
    ys = rows // (2 * coils)
    flat = lax.dot_general(table_ref[...], grid_ref[0], NT_DIMS, preferred_element_type=jnp.float32)
    flat = flat.reshape(ys, 2, coils, depth)
    real, imag = flat[:, 0], flat[:, 1]
    turn_re = turn_ref[0, 0][:, None, :]
    turn_im = turn_ref[0, 1][:, None, :]
    done_re = real * turn_re - imag * turn_im
    done_im = real * turn_im + imag * turn_re
    both = jnp.concatenate([done_re[:, None], done_im[:, None]], axis=1)
    out_ref[0] = both.reshape(rows, depth).astype(jnp.bfloat16)


def transform_columns(grids, table, turns, coils, chunk):
    tiles, depth, width = grids.shape
    rows = table.shape[0]
    ys = rows // (2 * coils)
    per = depth // chunk
    return pl.pallas_call(
        functools.partial(columns_kernel, coils),
        grid=(tiles, per),
        in_specs=[
            pl.BlockSpec((1, chunk, width), lambda t, k: (t, k, 0)),
            pl.BlockSpec((rows, width), lambda t, k: (0, 0)),
            pl.BlockSpec((1, 2, ys, chunk), lambda t, k: (t, 0, 0, k)),
        ],
        out_specs=pl.BlockSpec((1, rows, chunk), lambda t, k: (t, 0, k)),
        out_shape=jax.ShapeDtypeStruct((tiles, rows, depth), jnp.bfloat16),
        compiler_params=pltpu.CompilerParams(vmem_limit_bytes=40 << 20),
        name="transform_columns",
    )(grids, table, turns)


def image_kernel(blocks, ranks, coils, near, ys_step, *refs):
    mids = refs[:near]
    metas = refs[near : 2 * near]
    wave_ref, out_ref, held = refs[2 * near :]
    step = pl.program_id(0)
    rows, depth = mids[0].shape[1:]
    groups = rows // coils

    @pl.when(step < blocks)
    def _():
        lane = lax.broadcasted_iota(jnp.int32, (depth, LANES), 1).astype(jnp.float32)
        base = (step * LANES).astype(jnp.float32)
        hits = [meta[0][:, META_KX : META_KX + 1] - base == lane for meta in metas]
        for pair in range(ranks // 2):
            total = None
            for d in range(near):
                pick = [
                    jnp.where(hits[d], metas[d][0][:, 2 * pair + e : 2 * pair + e + 1], 0.0).astype(jnp.bfloat16)
                    for e in range(2)
                ]
                part = jnp.dot(mids[d][0], jnp.concatenate(pick, axis=1), preferred_element_type=jnp.float32)
                total = part if total is None else total + part
            low = total[:, :LANES].reshape(groups, 1, coils, LANES)
            high = total[:, LANES:].reshape(groups, 1, coils, LANES)
            both = jnp.concatenate([low, high], axis=1).reshape(groups, 2 * coils, LANES)
            held[:, pair, :, pl.ds(pl.multiple_of(step * LANES, LANES), LANES)] = both.astype(jnp.bfloat16)

    @pl.when(step >= blocks)
    def _():
        first = (step - blocks) * (2 * ys_step)
        block = held[pl.ds(first, 2 * ys_step)]
        plane = block.shape[-1]
        block = block.reshape(ys_step, 2, ranks * coils, plane)
        real, imag = block[:, 0:1], block[:, 1:2]
        straight = block.reshape(ys_step * 2 * ranks * coils, plane)
        crossed = jnp.concatenate([-imag, real], axis=1).reshape(ys_step * 2 * ranks * coils, plane)
        total = lax.dot_general(
            wave_ref[...], jnp.concatenate([straight, crossed], axis=1), NT_DIMS,
            preferred_element_type=jnp.float32,
        )
        out_ref[...] = (total * (1.0 / plane)).astype(jnp.bfloat16)


def form_image(mid, meta, wave, ranks, coils, tile_rows):
    tiles, rows, depth = mid.shape
    plane = wave.shape[0]
    blocks = plane // LANES
    firsts = [(b * LANES - 2) // tile_rows for b in range(blocks)]
    lasts = [(b * LANES + LANES + 1) // tile_rows for b in range(blocks)]
    near = max(last - first + 1 for first, last in zip(firsts, lasts))
    ys = rows // (2 * coils)
    ys_step = 4
    columns = ys_step * 2 * ranks * coils

    def tile_at(d):
        def at(s):
            b = jnp.minimum(s, blocks - 1)
            return ((b * LANES - 2 + tiles * tile_rows) // tile_rows + d) % tiles

        return at

    mid_specs = [pl.BlockSpec((1, rows, depth), lambda s, at=tile_at(d): (at(s), 0, 0)) for d in range(near)]
    meta_specs = [pl.BlockSpec((1, depth, LANES), lambda s, at=tile_at(d): (at(s), 0, 0)) for d in range(near)]
    return pl.pallas_call(
        functools.partial(image_kernel, blocks, ranks, coils, near, ys_step),
        grid=(blocks + ys // ys_step,),
        in_specs=[*mid_specs, *meta_specs, pl.BlockSpec((plane, 2 * plane), lambda s: (0, 0))],
        out_specs=pl.BlockSpec((plane, columns), lambda s: (0, jnp.maximum(s - blocks, 0))),
        out_shape=jax.ShapeDtypeStruct((plane, ys * 2 * ranks * coils), jnp.bfloat16),
        scratch_shapes=[pltpu.VMEM((rows // coils, ranks // 2, 2 * coils, plane), jnp.bfloat16)],
        compiler_params=pltpu.CompilerParams(vmem_limit_bytes=60 << 20),
        name="form_image",
    )(*([mid] * near), *([meta] * near), wave)


def body(coil_data, frame_of, basis, sample_pos, window_at, live_count):
    parts = coil_data.shape[2]
    tiles = coil_data.shape[3]
    slots = coil_data.shape[4]
    pair = coil_data.shape[5]
    samples = coil_data.shape[6]
    coils = pair // 2
    ranks = basis.shape[1]
    tile_rows = PLANE // tiles
    devices = parts * tiles
    count = devices * slots
    depth = count * WIN_ROWS
    my_part = lax.axis_index("kz")
    my_tile = lax.axis_index("tile")
    every = ("kz", "tile")

    raw = lax.all_to_all(
        coil_data.reshape(devices, slots * pair, samples), every, split_axis=0, concat_axis=0, tiled=True
    )
    counts = live_count.reshape(devices)
    slot_idx = jnp.arange(slots, dtype=jnp.int32)
    alive = (slot_idx[None, :] < counts[:, None]).astype(jnp.float32).reshape(count)
    windows = grid_windows(raw.reshape(count, pair, samples), sample_pos.reshape(count, 2, samples), alive)
    grids = lax.all_gather(windows, "tile", axis=0, tiled=False)

    notes = jnp.concatenate([frame_of.reshape(-1), window_at.reshape(-1)])
    notes = lax.all_gather(notes, every, axis=0, tiled=False)
    frames = notes[:, :count].reshape(devices, parts, tiles, slots)
    frames = lax.dynamic_index_in_dim(frames, my_part, 1, False)
    frames = jnp.transpose(frames, (1, 0, 2)).reshape(tiles, count)
    corners = lax.dynamic_slice_in_dim(notes[:, count:].reshape(parts, tiles, count, 2), my_part, 1, 0)[0]
    tile_idx = jnp.arange(tiles, dtype=jnp.int32)
    win_row = jnp.arange(WIN_ROWS, dtype=jnp.int32)
    kx = (tile_idx[:, None, None] * tile_rows + corners[:, :, 0:1] + win_row + PLANE) % PLANE
    kx = kx.reshape(tiles, depth, 1).astype(jnp.float32)
    coeff = jnp.repeat(basis[frames].astype(jnp.float32), WIN_ROWS, axis=1)
    meta = jnp.concatenate(
        [
            jnp.pad(coeff, ((0, 0), (0, 0), (0, META_KX - ranks))),
            jnp.pad(kx, ((0, 0), (0, 0), (0, LANES - META_KX - 1))),
        ],
        axis=2,
    )

    ys = PLANE // tiles
    y = my_tile * ys + jnp.arange(ys, dtype=jnp.int32)
    col0 = jnp.repeat(corners[:, :, 1], WIN_ROWS, axis=1)
    turn = phase_of(col0[:, None, :] * y[None, :, None])
    turns = jnp.stack([jnp.cos(turn), jnp.sin(turn)], axis=1)
    part = jnp.arange(2, dtype=jnp.int32)
    coil = jnp.arange(coils, dtype=jnp.int32)
    win_col = jnp.arange(WIN_COLS, dtype=jnp.int32)
    angle = phase_of(y[:, None] * win_col[None, :])
    cos_y, sin_y = jnp.cos(angle), jnp.sin(angle)
    mix = jnp.stack([jnp.stack([cos_y, -sin_y], axis=-1), jnp.stack([sin_y, cos_y], axis=-1)], axis=1)
    same = (coil[:, None] == coil[None, :]).astype(jnp.float32)
    table = mix[:, :, None, :, :, None] * same[None, None, :, None, None, :]
    table = table.reshape(ys * 2 * coils, WIN_COLS * pair).astype(jnp.bfloat16)
    index = jnp.arange(PLANE, dtype=jnp.int32)
    angle = phase_of(index[:, None] * index[None, :])
    wave = jnp.concatenate([jnp.cos(angle), jnp.sin(angle)], axis=1).astype(jnp.bfloat16)

    mid = transform_columns(grids, table, turns, coils, min(depth, 256))
    image = form_image(mid, meta, wave, ranks, coils, tile_rows)
    return image[None]


def solution(mesh):
    return jax.shard_map(
        body,
        mesh=mesh,
        in_specs=(
            P("kz", "tile", None, None, None, None, None),
            P("kz", "tile", None, None, None),
            P(),
            P("kz", "tile", None, None, None, None, None),
            P("kz", "tile", None, None, None, None),
            P("kz", "tile", None, None),
        ),
        out_specs=P("kz", None, "tile"),
        check_vma=False,
    )
```

time: 1170 us -> 208 us (0.18)
  blocking collectives: 572 us -> 40.6 us
  local copies, waits for them, and re-layouts: 243 us -> 43.8 us
  other arithmetic: 178 us -> 37.1 us
  matrix products: 127 us -> 0 us
  Pallas kernels: 0 us -> 64.1 us
  waiting for transfers between devices: 15 us -> 0.02 us
  starting transfers between devices: 22.3 us -> 7.37 us
  between operations: 0.66 us -> 13.7 us
    all_to_all x1 -> x0, blocking collectives: 572 us -> none  [body(): lax.all_to_all(mid, 'tile', split_axis=1, concat_axis=0, tiled=True)]
    unnamed x4 -> x0, matrix products: 122 us -> none
    slice x6 -> x5, local copies, waits for them, and re-layouts: 94.9 us -> 0.26 us  [the longest x2 0.17 us: body(): notes[:, count:].reshape(parts, tiles, count, 2)]
    unnamed x4 -> x1, other arithmetic: 67 us -> 0.19 us
    pallas_call x0 -> x3, Pallas kernels: none -> 64.1 us  [the longest x1 50.2 us: form_image(): pl.pallas_call(functools.partial(image_kernel, blocks, ranks, coils, near...]
    unnamed x0 -> x1, blocking collectives: none -> 40.6 us
    concatenate x1 -> x0, local copies, waits for them, and re-layouts: 38.3 us -> none  [combine(): jnp.concatenate([first[..., :half] - second[..., half:], second[..., :hal...]
    all_to_all x5 -> x0, local copies, waits for them, and re-layouts: 37.6 us -> none  [the longest x1 36 us: body(): lax.all_to_all(mid, 'tile', split_axis=1, concat_axis=0, tiled=True)]
  transfers between devices with their start and end apart: 6 -> 2, of which waited for: 3 -> 0; matrix products, arithmetic and copies ran while one was open for 9% -> 37% of each run, Pallas kernels for 0% -> 0%
where the time goes in v1:
time: 208 us; the launch traced here: 207 us
  Pallas kernels  64.1 us (31%)
  local copies, waits for them, and re-layouts  43.8 us (21%)
  blocking collectives  40.6 us (20%)
  other arithmetic  37.1 us (18%)
  between operations  13.7 us (7%)
  starting transfers between devices  7.37 us (4%)
    pallas_call x1, Pallas kernels, form_image(): pl.pallas_call(functools.partial(image_kernel, blocks, ranks, coils, near...  50.2 us
    unnamed x1, blocking collectives  40.6 us
    convert_element_type x1, local copies, waits for them, and re-layouts, body(): table = table.reshape(ys * 2 * coils, WIN_COLS * pair).astype(jnp.bfloat16)  30.4 us
    convert_element_type x1, other arithmetic, body(): table = table.reshape(ys * 2 * coils, WIN_COLS * pair).astype(jnp.bfloat16)  23.6 us
    pallas_call x1, Pallas kernels, grid_windows(): pl.pallas_call(functools.partial(window_kernel, quad), grid=(count // qua...  9.59 us
    all_to_all x1, starting transfers between devices, body(): lax.all_to_all(coil_data.reshape(devices, slots * pair, samples), every,...  7.33 us
    another operation x1, other arithmetic  6.92 us
    unnamed x16, local copies, waits for them, and re-layouts  5.75 us
  transfers between devices with their start and end apart: 2, of which 0 were waited for; matrix products, arithmetic and copies ran while one was open for 37% of the time, Pallas kernels for 0%

profile of v1, /device:TPU:0, one launch (start us, length us, event | category | flops | bytes accessed | tf_op | source)
XLA Modules:
  0.0 206.7 jit_solution(17068504455020385335)
XLA Ops:
  6.5 7.3 %all-to-all-start = ((bf16[32,32,128]{2,1,0:T(8,128)(2,1)}), bf16[32,32,128]{2,1,0:T(8,128)(2,1)S(1)}, u32[]{:S(2)}, u32[]{:S(2)}) async-start(bf16[32,32,128]{2,1,0:T(8,128)(2,1)} %bitcast.36), calls=%async_computation | async-start | bytes 524288 | tf_op jit(solution)/shard_map/all_to_all | solution.py:192
  13.9 0.8 copy.42
  14.9 0.8 copy.41
  15.8 0.2 add_dynamic-update-slice_fusion
  16.0 40.6 %all-reduce.2 = s32[6144]{0:T(1024)S(1)} all-reduce(s32[6144]{0:T(1024)S(1)} %add_dynamic-update-slice_fusion), channel_id=3, replica_groups=mesh['kz'=4,'tile'=8] {'kz','tile'}, use_global_device_ids=true, to_apply=%add.2 | all-reduce | flops 6144 | bytes 49152
  56.8 0.2 reshape.326
  57.4 2.4 %copy.40 = f32[80,2,32,2]{3,2,1,0:T(8,128)S(1)} copy(f32[80,2,32,2]{0,2,3,1:T(8,128)S(1)} %pad_maximum_fusion.2) | data formatting | bytes 81920 | tf_op jit(solution)/shard_map/stack | solution.py:230
  60.1 0.7 broadcast_in_dim.8.alive_ref
  60.9 9.6 %grid_windows.1 = bf16[256,512]{1,0:T(8,128)(2,1)} custom-call(bf16[64,16,128]{2,1,0:T(8,128)(2,1)} %bitcast.32, f32[64,2,128]{2,1,0:T(2,128)} %bitcast.41, f32[64,1,128]{2,1,0:T(1,128)} %broadcast_in_dim.8.alive_ref), custom_call_target="tpu_custom_call" | custom-call | tf_op jit(solution)/shard_map/grid_windows/pallas_call | solution.py:52
  70.5 23.6 %multiply_convert_fusion = bf16[80,2,8,32,2,8]{5,4,3,2,1,0:T(2,128)(2,1)} fusion(f32[8,8]{1,0:T(8,128)S(1)} %fusion.22, f32[80,2,32,2]{3,2,1,0:T(8,128)S(1)} %copy.40), kind=kLoop, calls=%fused_computation.1 | loop fusion | flops 1310720 | bytes 1351936 | tf_op jit(solution)/shard_map/convert_element_type | solution.py:233
  94.1 30.4 %convert_element_type.83.table_ref = bf16[1280,512]{1,0:T(8,128)(2,1)S(1)} reshape(bf16[80,2,8,32,2,8]{5,4,3,2,1,0:T(2,128)(2,1)} %multiply_convert_fusion) | data formatting | bytes 2621440 | tf_op jit(solution)/shard_map/convert_element_type | solution.py:233
  124.5 1.6 copy.50
  126.6 0.2 copy.49
  126.8 1.3 gather_fusion
  128.2 0.7 fusion.5
  128.9 0.2 broadcast_in_dim.10
  129.0 1.3 select_maximum_fusion.refs_3_.refs_4_.refs_5_
  130.3 2.7 %fusion.11 = (f32[8,1,80,256]{3,2,1,0:T(8,128)S(1)}, f32[8,1,80,256]{3,2,1,0:T(8,128)S(1)}) fusion(s32[80]{0:T(128)S(1)} %iota_add_fusion, s32[8,256]{1,0:T(8,128)S(1)} %copy.44), kind=kLoop, calls=%fused_computation.26 | loop fusion | flops 1474560 | bytes 1319232 | tf_op jit(solution)/shard_map/cos | solution.py:224
  133.2 6.9 %sine_convert_fusion = (bf16[640,640]{1,0:T(8,128)(2,1)S(1)}, bf16[640,640]{1,0:T(8,128)(2,1)S(1)}) fusion(), kind=kLoop, calls=%fused_computation.6 | loop fusion | flops 4505600 | bytes 1638400 | tf_op jit(solution)/shard_map/convert.2
  140.1 1.3 pad_maximum_fusion.refs_6_
  141.4 1.6 copy-done.1
  143.0 4.3 %transform_columns.1.refs_0_.refs_1_.refs_2_ = bf16[8,1280,256]{2,1,0:T(8,128)(2,1)S(1)} custom-call(bf16[8,256,512]{2,1,0:T(8,128)(2,1)S(1)} %bitcast.30, bf16[1280,512]{1,0:T(8,128)(2,1)S(1)} %convert_element_type.83.table_ref, f32[8,2,80,256]{3,2,1,0:T(8,128)S(1)} %pad_maximum_fusion.1.turn_ref), custom_call_target="tpu_custom_call" | custom-call | tf_op jit(solution)/shard_map/transform_columns/pallas_call | solution.py:86
  147.3 2.3 %copy-done = bf16[8,1280,256]{2,1,0:T(8,128)(2,1)} copy-done((bf16[8,1280,256]{2,1,0:T(8,128)(2,1)}, bf16[8,1280,256]{2,1,0:T(8,128)(2,1)S(1)}, u32[]{:S(2)}) %copy-start) | copy-done | bytes 5242904
  149.6 50.2 %form_image.1 = bf16[640,12800]{1,0:T(8,128)(2,1)} custom-call(bf16[8,1280,256]{2,1,0:T(8,128)(2,1)} %copy-done, bf16[8,1280,256]{2,1,0:T(8,128)(2,1)} %copy-done, bf16[8,1280,256]{2,1,0:T(8,128)(2,1)} %copy-done, f32[8,256,128]{2,1,0:T(8,128)} %select_maximum_fusion.refs_3_.refs_4_.refs_5_, f32[8,256,128]{2,1,0:T(8,128)} %select_maximum_fusion.refs_3_.refs_4_.refs_5_, ...), custom_call_target="tpu_custom_call" | custom-call | tf_op jit(solution)/shard_map/form_image/pallas_call | solution.py:164
  (47 shorter events, 1.7 us)
Async XLA Ops:
  6.5 53.6 %all-to-all-start = ((bf16[32,32,128]{2,1,0:T(8,128)(2,1)}), bf16[32,32,128]{2,1,0:T(8,128)(2,1)S(1)}, u32[]{:S(2)}, u32[]{:S(2)}) async-start(bf16[32,32,128]{2,1,0:T(8,128)(2,1)} %bitcast.36), calls=%async_computation | async-start | bytes 524288 | tf_op jit(solution)/shard_map/all_to_all | solution.py:192
  13.9 127.5 %all-gather.4.cloned.1.call-start = ((), (), s32[]{:S(2)}) async-start(), calls=%async_computation.1 | async-start | bytes 2359296 | tf_op jit(solution)/shard_map/all_gather | solution.py:199
  56.7 3.1 %copy-start.3 = (s32[32,192]{1,0:T(8,128)}, s32[32,192]{1,0:T(8,128)S(1)}, u32[]{:S(2)}) copy-start(s32[32,192]{1,0:T(8,128)S(1)} %reshape.340) | copy-start | bytes 73732
  57.1 2.7 %copy-start.5 = (s32[1,1,4,8]{3,2,1,0:T(4,128)S(1)}, s32[1,1,4,8]{3,2,1,0:T(4,128)}, u32[]{:S(2)}) copy-start(s32[1,1,4,8]{3,2,1,0:T(4,128)} %param.11) | copy-start | bytes 388
  60.1 0.7 copy-start.2
  94.1 32.2 %slice-start = ((s32[32,192]{1,0:T(8,128)}), s32[32,64]{1,0:T(8,128)S(1)}, s32[]{:S(2)}) async-start(s32[32,192]{1,0:T(8,128)} %copy-done.3), calls=%async_computation.2 | async-start | bytes 32768 | tf_op jit(solution)/shard_map/slice | solution.py:203
  124.5 2.1 %copy-start.4 = (bf16[1000,10]{0,1:T(8,128)(2,1)S(1)}, bf16[1000,10]{0,1:T(8,128)(2,1)}, u32[]{:S(2)}) copy-start(bf16[1000,10]{0,1:T(8,128)(2,1)} %param.8) | copy-start | bytes 60004
  141.4 1.6 copy-start.1
  147.3 2.3 %copy-start = (bf16[8,1280,256]{2,1,0:T(8,128)(2,1)}, bf16[8,1280,256]{2,1,0:T(8,128)(2,1)S(1)}, u32[]{:S(2)}) copy-start(bf16[8,1280,256]{2,1,0:T(8,128)(2,1)S(1)} %transform_columns.1.refs_0_.refs_1_.refs_2_) | copy-start | bytes 15728644
Sparse Core Ops, SparseCore 0:
  70.6 48.9 all-gather.3
